TPU v7x, 128 devices: a whole 4x4x4 slice. The times are simulated.
128 devices in a mesh: cent: 4 (over y), rows: 32 (over z, x, core).
Axes of the slice: x: 4, y: 4, z: 4, core: 2. Of those that a mesh axis runs over, the one named last changes fastest.
Arguments:
- embeddings: bfloat16 [32768, 2048], P(('cent', 'rows')), may hold values from -6 to 6
- centroids: bfloat16 [16384, 2048], P(('cent', 'rows')), may hold values from -0.125 to 0.125
- cluster: int32 [32768, 1], P(('cent', 'rows')), may hold values from 0 to 127; in each aligned block of 256 rows (0 to 255, 256 to 511, ...) at most 4 rows name the same one
- noise_salt: int32 [1], replicated, may hold values from 0 to 1048575
Outputs:
- perturbed_max: float32 [32768], P(('cent', 'rows'))
- dedup_score: float32 [32768], P(('cent', 'rows'))
- new_centroids: float32 [128, 2048], P(('cent', 'rows'))
Inputs may be any that keep to these rules, and one draw needn't show every extreme that they name: In every aligned block of 256 rows (the rows of one device) no cluster is named by more than 4 rows, and in some block some cluster by exactly 4; every cluster is named by some row.
All inputs are finite; a program needn't handle non-finite values.
Results may differ from a plain program's by a relative error of at most 0.0003.
Values may be sent and summed in bfloat16 or wider, within the bound.
A program may use at most 128 MiB of HBM per device.

v0:
```python
import math
import jax
import jax.numpy as jnp
from jax import lax
from jax.sharding import Mesh
from jax.sharding import PartitionSpec as P

inverse_temp = 3.0
epsilon = 1e-06
ALL = ("y", "z", "x", "c")


def logical_shift(word, amount):
    return lax.shift_right_logical(word, jnp.full(word.shape, amount, jnp.int32))


def gumbel_noise(row_ids, cent_ids, salt_word):
    mixed = row_ids * 1103515245 + cent_ids * 739982445 + salt_word
    mixed = mixed ^ logical_shift(mixed, 16)
    mixed = mixed * 2146121005
    mixed = mixed ^ logical_shift(mixed, 15)
    mixed = mixed * 1759714725
    mixed = mixed ^ logical_shift(mixed, 16)
    low_bits = mixed & 8388607
    uniform = (low_bits.astype(jnp.float32) + 0.5) * (1.0 / 8388608.0)
    return -jnp.log(-jnp.log(uniform))


def cluster_stats(members, valid):
    feature_dim = members.shape[1]
    widened = members.astype(jnp.float32)
    scale = lax.rsqrt(jnp.mean(widened * widened, axis=1) + epsilon)
    gram = lax.dot_general(
        members, members, (((1,), (1,)), ((), ())), preferred_element_type=jnp.float32
    )
    similar = gram * scale[:, None] * scale[None, :] * (1.0 / math.sqrt(feature_dim))
    order = jnp.arange(members.shape[0], dtype=jnp.int32)
    usable = valid[None, :] & (order[:, None] != order[None, :])
    highest = jnp.max(jnp.where(usable, similar, -1e30), axis=1)
    scores = jnp.where(jnp.any(usable, axis=1), highest, 0.0)
    total = jnp.sum(jnp.where(valid[:, None], widened, 0.0), axis=0)
    center = total * lax.rsqrt(jnp.mean(total * total) + epsilon)
    return (scores, center)


def shards(embeddings, centroids, cluster, noise_salt):
    rows_dev, feature_dim = embeddings.shape
    cent_dev = centroids.shape[0]
    ny, nz, nx, nc = (lax.axis_size(a) for a in ALL)
    devices = ny * nz * nx * nc
    capacity = max(2, 2 * rows_dev // devices)
    iy, iz, ix, ic = (lax.axis_index(a) for a in ALL)
    me = ((iy * nz + iz) * nx + ix) * nc + ic
    salt_word = noise_salt[0]
    group = lax.all_gather(
        lax.all_gather(embeddings, "y", axis=0, tiled=True), "c", axis=0, tiled=True
    )
    piece = lax.all_gather(centroids, ("z", "x"), axis=0, tiled=True)
    position = jnp.arange(nc * ny * rows_dev, dtype=jnp.int32)
    src_c = position // (ny * rows_dev)
    src_y = position // rows_dev % ny
    row_dev = ((src_y * nz + iz) * nx + ix) * nc + src_c
    group_ids = row_dev * rows_dev + position % rows_dev
    cpos = jnp.arange(nz * nx * cent_dev, dtype=jnp.int32)
    cent_dev_ids = ((iy * nz + cpos // (nx * cent_dev)) * nx + cpos // cent_dev % nx) * nc + ic
    cent_ids = cent_dev_ids * cent_dev + cpos % cent_dev
    piece_rows = piece.shape[0]
    block = math.gcd(piece_rows, 512)
    steps = piece_rows // block
    tiles = piece.reshape(steps, block, feature_dim)
    noise = gumbel_noise(group_ids[:, None], cent_ids[None, :], salt_word)
    noise_tiles = noise.reshape(group.shape[0], steps, block).transpose(1, 0, 2)
    initial = jnp.full((group.shape[0],), -1e30, jnp.float32)

    def step(carry, item):
        tile, noise_tile = item
        scores = lax.dot_general(
            group, tile, (((1,), (1,)), ((), ())), preferred_element_type=jnp.float32
        )
        perturbed = inverse_temp * scores + noise_tile
        return (jnp.maximum(carry, jnp.max(perturbed, axis=1)), None)

    result, unused = lax.scan(step, initial, (tiles, noise_tiles))
    merged = lax.pmax(result, ("c", "y"))
    perturbed_max = lax.dynamic_slice_in_dim(merged, (ic * ny + iy) * rows_dev, rows_dev)
    assigned = cluster[:, 0]
    order = jnp.arange(rows_dev, dtype=jnp.int32)
    same = (assigned[:, None] == assigned[None, :]) & (order[None, :] < order[:, None])
    rank = jnp.sum(same.astype(jnp.int32), axis=1)
    slot = assigned * capacity + rank
    outgoing = jnp.zeros((devices * capacity, feature_dim), jnp.bfloat16).at[slot].set(embeddings)
    present = (
        jnp.zeros((devices * capacity,), jnp.bfloat16)
        .at[slot]
        .set(jnp.ones((rows_dev,), jnp.bfloat16))
    )
    received = lax.all_to_all(
        outgoing.reshape(devices, capacity, feature_dim),
        ALL,
        split_axis=0,
        concat_axis=0,
        tiled=True,
    )
    arrived = lax.all_to_all(
        present.reshape(devices, capacity), ALL, split_axis=0, concat_axis=0, tiled=True
    )
    members = received.reshape(devices * capacity, feature_dim)
    valid = arrived.reshape(devices * capacity) > 0.5
    scores, center = cluster_stats(members, valid)
    returned = lax.all_to_all(
        scores.reshape(devices, capacity), ALL, split_axis=0, concat_axis=0, tiled=True
    )
    dedup_score = returned.reshape(devices * capacity)[slot]
    return (perturbed_max, dedup_score, center[None, :])


def solution(mesh):
    cent_count, rows_count = mesh.devices.shape
    cores = 2
    side = math.isqrt(rows_count // cores)
    view = Mesh(mesh.devices.reshape(cent_count, side, rows_count // cores // side, cores), ALL)
    spec = P(ALL, None)
    in_specs = (spec, spec, spec, P())
    out_specs = (P(ALL), P(ALL), spec)
    return jax.shard_map(shards, mesh=view, in_specs=in_specs, out_specs=out_specs, check_vma=False)
```

profile of v0, /device:TPU:1, one launch (start us, length us, event | category | flops | bytes accessed | tf_op | source)
XLA Modules:
  0.0 235.4 jit_solution(165970841655316677)
XLA Ops:
  7.9 53.2 %all-gather.6.cloned.1.call-done = bf16[1024,2048]{1,0:T(8,128)(2,1)} async-done(((bf16[256,2048]{1,0:T(8,128)(2,1)}), bf16[1024,2048]{1,0:T(8,128)(2,1)}) %all-gather.6.cloned.1.call-update) | async-done | bytes 4194320 | tf_op jit(solution)/shard_map/all_gather | solution.py:56
  62.0 0.9 convert_reduce_fusion
  63.6 2.2 scatter_custom_fusion
  66.5 8.6 %all-to-all-start = ((bf16[128,1,4]{2,1,0:T(2,128)(2,1)}), bf16[128,1,4]{2,1,0:T(2,128)(2,1)S(1)}, u32[]{:S(2)}, u32[]{:S(2)}) async-start(bf16[128,1,4]{2,1,0:T(2,128)(2,1)} %all_to_all.17), calls=%async_computation | async-start | bytes 131072 | tf_op jit(solution)/shard_map/all_to_all | solution.py:104
  75.2 3.7 %scatter_custom_fusion.1 = bf16[512,2048]{1,0:T(8,128)(2,1)S(1)} fusion(s32[256]{0:T(256)S(1)} %bitcast.33, bf16[256,2048]{1,0:T(8,128)(2,1)} %param.6, bf16[]{:T(256)} %constant.177.clone.1), kind=kCustom, calls=%fused_computation.31 | custom fusion | bytes 2097664 | tf_op jit(solution)/shard_map/scatter | solution.py:91
  79.6 2.2 reshape.217
  81.8 2.8 %all-to-all-done = bf16[128,1,4]{2,1,0:T(2,128)(2,1)S(1)} async-done(((bf16[128,1,4]{2,1,0:T(2,128)(2,1)}), bf16[128,1,4]{2,1,0:T(2,128)(2,1)S(1)}, u32[]{:S(2)}, u32[]{:S(2)}) %all-to-all-start) | async-done | bytes 1056 | tf_op jit(solution)/shard_map/all_to_all | solution.py:104
  84.6 6.9 %all-to-all-start.1 = ((bf16[128,4,2048]{2,1,0:T(4,128)(2,1)}), bf16[128,4,2048]{2,1,0:T(4,128)(2,1)S(1)}, u32[]{:S(2)}, u32[]{:S(2)}) async-start(bf16[128,4,2048]{2,1,0:T(4,128)(2,1)} %reshape.217), calls=%async_computation.1 | async-start | bytes 4194304 | tf_op jit(solution)/shard_map/all_to_all | solution.py:97
  91.5 12.2 %fusion.13 = f32[4,2048,512]{1,2,0:T(8,128)} fusion(s32[]{:T(128)} %bitcast.28, s32[4,512]{1,0:T(4,128)S(1)} %fusion.55, s32[2048]{0:T(1024)S(1)} %fusion.40), kind=kLoop, calls=%fused_computation.21 | loop fusion | flops 67108864 | bytes 16793604 | tf_op jit(solution)/shard_map/neg | solution.py:26
  104.5 25.5 %all-to-all-done.1 = bf16[128,4,2048]{2,1,0:T(4,128)(2,1)S(1)} async-done(((bf16[128,4,2048]{2,1,0:T(4,128)(2,1)}), bf16[128,4,2048]{2,1,0:T(4,128)(2,1)S(1)}, u32[]{:S(2)}, u32[]{:S(2)}) %all-to-all-start.1) | async-done | bytes 2097184 | tf_op jit(solution)/shard_map/all_to_all | solution.py:97
  130.0 2.1 fusion.15
  132.2 2.0 reshape.218
  134.3 4.3 %fusion.19 = f32[512]{0:T(512)S(1)} fusion(bf16[512,2048]{1,0:T(8,128)(2,1)} %reshape.218, f32[512]{0:T(512)S(1)} %rsqrt.18, pred[512]{0:T(512)(128)(4,1)S(1)} %gt.22), kind=kOutput, calls=%fused_computation.30 | convolution fusion | flops 1075576320 | bytes 2101760 | tf_op jit(solution)/shard_map/dot_general | solution.py:33
  139.3 4.5 %all-to-all-start.2 = ((f32[128,1,4]{2,1,0:T(1,128)}), f32[128,1,4]{2,1,0:T(1,128)S(1)}, u32[]{:S(2)}, u32[]{:S(2)}) async-start(f32[128,1,4]{2,1,0:T(1,128)} %bitcast.5), calls=%async_computation.2 | async-start | bytes 131072 | tf_op jit(solution)/shard_map/all_to_all | solution.py:110
  145.7 8.0 %all-to-all-done.2 = f32[128,1,4]{2,1,0:T(1,128)S(1)} async-done(((f32[128,1,4]{2,1,0:T(1,128)}), f32[128,1,4]{2,1,0:T(1,128)S(1)}, u32[]{:S(2)}, u32[]{:S(2)}) %all-to-all-start.2) | async-done | bytes 2080 | tf_op jit(solution)/shard_map/all_to_all | solution.py:110
  154.3 0.8 reduce.7
  155.2 2.5 %gather_fusion = f32[256]{0:T(256)} fusion(f32[512]{0:T(512)S(1)} %reshape.219, s32[1024]{0:T(1024)S(1)} %pad_clamp_fusion), kind=kCustom, calls=%fused_computation | custom fusion | bytes 3072 | tf_op jit(solution)/shard_map/gather | solution.py:113
  157.7 15.8 %all-gather.4.cloned.1.call-done = bf16[2048,2048]{1,0:T(8,128)(2,1)} async-done(((bf16[128,2048]{1,0:T(8,128)(2,1)}), bf16[2048,2048]{1,0:T(8,128)(2,1)}) %all-gather.4.cloned.1.call-update) | async-done | bytes 8388624 | tf_op jit(solution)/shard_map/all_gather | solution.py:58
  173.5 39.0 %while.11 = (s32[]{:T(128)}, f32[2048]{0:T(1024)S(1)}, bf16[4,512,2048]{2,1,0:T(8,128)(2,1)}, bf16[2048,2048]{1,0:T(8,128)(2,1)}, f32[4,2048,512]{1,2,0:T(8,128)}, /*index=5*/s32[]{:T(128)}, s32[]{:T(128)}) while((s32[]{:T(128)}, f32[2048]{0:T(1024)S(1)}, bf16[4,512,2048]{2,1,0:T(8,128)(2,1)}, bf16[2048,2048]{1,0:T(8,128)(2,1)}, ...), condition=%wide.region_2.3_spmd.clone, body=%wide.region_0.2_spmd.clone.sunk | while | flops 4298115072 | bytes 14713943 | solution.py:83
  173.5 9.7 %fusion.69 = f32[2048]{0:T(1024)S(1)} fusion(f32[4,2048,512]{1,2,0:T(8,128)} %get-tuple-element.112, s32[]{:T(128)} %get-tuple-element.101, bf16[2048,2048]{1,0:T(8,128)(2,1)} %get-tuple-element.111, bf16[4,512,2048]{2,1,0:T(8,128)(2,1)} %get-tuple-element.110), kind=kOutput, calls=%fused_computation.4.clone.1 | convolution fusion | flops 4298110976 | bytes 14689280 | tf_op jit(solution)/shard_map/while/body/eval_jaxpr/dot_general | solution.py:77
  183.2 9.7 %fusion.69 = f32[2048]{0:T(1024)S(1)} fusion(f32[4,2048,512]{1,2,0:T(8,128)} %get-tuple-element.112, s32[]{:T(128)} %get-tuple-element.101, bf16[2048,2048]{1,0:T(8,128)(2,1)} %get-tuple-element.111, bf16[4,512,2048]{2,1,0:T(8,128)(2,1)} %get-tuple-element.110), kind=kOutput, calls=%fused_computation.4.clone.1 | convolution fusion | flops 4298110976 | bytes 14689280 | tf_op jit(solution)/shard_map/while/body/eval_jaxpr/dot_general | solution.py:77
  193.0 9.7 %fusion.69 = f32[2048]{0:T(1024)S(1)} fusion(f32[4,2048,512]{1,2,0:T(8,128)} %get-tuple-element.112, s32[]{:T(128)} %get-tuple-element.101, bf16[2048,2048]{1,0:T(8,128)(2,1)} %get-tuple-element.111, bf16[4,512,2048]{2,1,0:T(8,128)(2,1)} %get-tuple-element.110), kind=kOutput, calls=%fused_computation.4.clone.1 | convolution fusion | flops 4298110976 | bytes 14689280 | tf_op jit(solution)/shard_map/while/body/eval_jaxpr/dot_general | solution.py:77
  202.7 9.7 %fusion.69 = f32[2048]{0:T(1024)S(1)} fusion(f32[4,2048,512]{1,2,0:T(8,128)} %get-tuple-element.112, s32[]{:T(128)} %get-tuple-element.101, bf16[2048,2048]{1,0:T(8,128)(2,1)} %get-tuple-element.111, bf16[4,512,2048]{2,1,0:T(8,128)(2,1)} %get-tuple-element.110), kind=kOutput, calls=%fused_computation.4.clone.1 | convolution fusion | flops 4298110976 | bytes 14689280 | tf_op jit(solution)/shard_map/while/body/eval_jaxpr/dot_general | solution.py:77
  212.5 15.8 %pmax.7 = f32[2048]{0:T(1024)S(1)} all-reduce(f32[2048]{0:T(1024)S(1)} %get-tuple-element.30), channel_id=1, replica_groups=mesh['y'=4,'z'=4,'x'=4,'c'=2] {'c','y'}, use_global_device_ids=true, to_apply=%region_3.4 | all-reduce | flops 2048 | bytes 16384 | tf_op jit(solution)/shard_map/pmax | solution.py:84
  (32 shorter events, 7.1 us)
Async XLA Ops:
  7.2 54.0 %all-gather.6.cloned.1.call-start = ((), (), s32[]{:S(2)}) async-start(), calls=%async_computation.4 | async-start | bytes 5242880 | tf_op jit(solution)/shard_map/all_gather | solution.py:56
  7.9 149.8 %all-gather.8.cloned.1.call-start = ((), (), s32[]{:S(2)}) async-start(), calls=%async_computation.5 | async-start | bytes 12582912 | tf_op jit(solution)/shard_map/all_gather | solution.py:55
  61.2 112.3 %all-gather.4.cloned.1.call-start = ((), (), s32[]{:S(2)}) async-start(), calls=%async_computation.3 | async-start | bytes 8912896 | tf_op jit(solution)/shard_map/all_gather | solution.py:58
  66.5 18.1 %all-to-all-start = ((bf16[128,1,4]{2,1,0:T(2,128)(2,1)}), bf16[128,1,4]{2,1,0:T(2,128)(2,1)S(1)}, u32[]{:S(2)}, u32[]{:S(2)}) async-start(bf16[128,1,4]{2,1,0:T(2,128)(2,1)} %all_to_all.17), calls=%async_computation | async-start | bytes 131072 | tf_op jit(solution)/shard_map/all_to_all | solution.py:104
  84.6 45.4 %all-to-all-start.1 = ((bf16[128,4,2048]{2,1,0:T(4,128)(2,1)}), bf16[128,4,2048]{2,1,0:T(4,128)(2,1)S(1)}, u32[]{:S(2)}, u32[]{:S(2)}) async-start(bf16[128,4,2048]{2,1,0:T(4,128)(2,1)} %reshape.217), calls=%async_computation.1 | async-start | bytes 4194304 | tf_op jit(solution)/shard_map/all_to_all | solution.py:97
  139.3 14.4 %all-to-all-start.2 = ((f32[128,1,4]{2,1,0:T(1,128)}), f32[128,1,4]{2,1,0:T(1,128)S(1)}, u32[]{:S(2)}, u32[]{:S(2)}) async-start(f32[128,1,4]{2,1,0:T(1,128)} %bitcast.5), calls=%async_computation.2 | async-start | bytes 131072 | tf_op jit(solution)/shard_map/all_to_all | solution.py:110
Sparse Core Ops, SparseCore 0:
  9.7 51.4 all-gather.5
  62.8 23.2 all-gather.7
  88.3 85.1 all-gather.3
where the time goes:
time: 236 us; the launch traced here: 235 us
  waiting for transfers between devices  107 us (45%)
  matrix products  43.1 us (18%)
  starting transfers between devices  20.1 us (9%)
  other arithmetic  18.5 us (8%)
  local copies, waits for them, and re-layouts  15.8 us (7%)
  blocking collectives  15.8 us (7%)
  between operations  15.2 us (6%)
    all_gather x1, waiting for transfers between devices, shards(): lax.all_gather(embeddings, 'y', axis=0, tiled=True)  53.2 us
    dot_general x4, matrix products, step(): lax.dot_general(group, tile, (((1,), (1,)), ((), ())), preferred_element_...  38.8 us
    all_to_all x1, waiting for transfers between devices, shards(): lax.all_to_all(outgoing.reshape(devices, capacity, feature_dim), ALL, spl...  25.5 us
    all_gather x1, waiting for transfers between devices, shards(): piece = lax.all_gather(centroids, ('z', 'x'), axis=0, tiled=True)  15.8 us
    pmax x1, blocking collectives, shards(): merged = lax.pmax(result, ('c', 'y'))  15.8 us
    neg x1, other arithmetic, gumbel_noise(): return -jnp.log(-jnp.log(uniform))  12.2 us
    all_to_all x1, starting transfers between devices, shards(): lax.all_to_all(present.reshape(devices, capacity), ALL, split_axis=0, con...  8.6 us
    all_to_all x1, waiting for transfers between devices, shards(): lax.all_to_all(scores.reshape(devices, capacity), ALL, split_axis=0, conc...  8.01 us
  transfers between devices with their start and end apart: 6, of which 5 were waited for; matrix products, arithmetic and copies ran while one was open for 16% of the time, Pallas kernels for 0%

commit v1 on v0

--- a/solution.py
+++ b/solution.py
@@ -55,7 +55,8 @@
     group = lax.all_gather(
         lax.all_gather(embeddings, "y", axis=0, tiled=True), "c", axis=0, tiled=True
     )
-    piece = lax.all_gather(centroids, ("z", "x"), axis=0, tiled=True)
+    repeated = jnp.stack([centroids] * lax.axis_size(("z", "x")))
+    piece = jnp.concatenate(lax.all_to_all(repeated, ("z", "x"), 0, 0), axis=0)
     position = jnp.arange(nc * ny * rows_dev, dtype=jnp.int32)
     src_c = position // (ny * rows_dev)
     src_y = position // rows_dev % ny

time: 236 us -> 300 us (1.27)
  waiting for transfers between devices: 107 us -> 148 us
  blocking collectives: 15.8 us -> 32.9 us
  local copies, waits for them, and re-layouts: 15.8 us -> 19.5 us
    all_to_all x1, waiting for transfers between devices: 8.01 us -> 104 us  [shards(): piece = jnp.concatenate(lax.all_to_all(repeated, ('z', 'x'), 0, 0), axis=0)]
    all_gather x1, waiting for transfers between devices: 53.2 us -> 6.47 us  [shards(): lax.all_gather(embeddings, 'y', axis=0, tiled=True)]
    all_to_all x0 -> x1, blocking collectives: none -> 17.8 us  [shards(): lax.all_to_all(scores.reshape(devices, capacity), ALL, split_axis=0, conc...]
    all_gather x1 -> x0, waiting for transfers between devices: 15.8 us -> none  [shards(): piece = lax.all_gather(centroids, ('z', 'x'), axis=0, tiled=True)]
    all_to_all x1, waiting for transfers between devices: 25.5 us -> 33.1 us  [shards(): lax.all_to_all(outgoing.reshape(devices, capacity, feature_dim), ALL, spl...]
    another operation x0 -> x1, local copies, waits for them, and re-layouts: none -> 4.29 us  [shards(): repeated = jnp.stack([centroids] * lax.axis_size(('z', 'x')))]
  transfers between devices with their start and end apart: 6 -> 5, of which waited for: 5 -> 4; matrix products, arithmetic and copies ran while one was open for 16% -> 13% of each run, Pallas kernels for 0% -> 0%
where the time goes in v1:
time: 300 us
  waiting for transfers between devices  148 us (49%)
  matrix products  42.4 us (14%)
  blocking collectives  32.9 us (11%)
  starting transfers between devices  22.7 us (8%)
  local copies, waits for them, and re-layouts  19.5 us (6%)
  other arithmetic  18.5 us (6%)
  between operations  15.5 us (5%)
    all_to_all x1, waiting for transfers between devices, shards(): piece = jnp.concatenate(lax.all_to_all(repeated, ('z', 'x'), 0, 0), axis=0)  104 us
    dot_general x4, matrix products, step(): lax.dot_general(group, tile, (((1,), (1,)), ((), ())), preferred_element_...  38.8 us
    all_to_all x1, waiting for transfers between devices, shards(): lax.all_to_all(outgoing.reshape(devices, capacity, feature_dim), ALL, spl...  33.1 us
    all_to_all x1, blocking collectives, shards(): lax.all_to_all(scores.reshape(devices, capacity), ALL, split_axis=0, conc...  17.8 us
    pmax x1, blocking collectives, shards(): merged = lax.pmax(result, ('c', 'y'))  15.2 us
    neg x1, other arithmetic, gumbel_noise(): return -jnp.log(-jnp.log(uniform))  12.2 us
    all_to_all x1, starting transfers between devices, shards(): lax.all_to_all(present.reshape(devices, capacity), ALL, split_axis=0, con...  11.5 us
    all_gather x1, waiting for transfers between devices, shards(): lax.all_gather(embeddings, 'y', axis=0, tiled=True)  6.47 us
  transfers between devices with their start and end apart: 5, of which 4 were waited for; matrix products, arithmetic and copies ran while one was open for 13% of the time, Pallas kernels for 0%

profile of v1, /device:TPU:1, one launch (start us, length us, event | category | flops | bytes accessed | tf_op | source)
XLA Modules:
  0.0 300.0 jit_solution(4422752879383560562)
XLA Ops:
  7.9 0.9 convert_reduce_fusion
  9.5 2.2 scatter_custom_fusion
  12.4 11.5 %all-to-all-start.1 = ((bf16[128,1,4]{2,1,0:T(2,128)(2,1)}), bf16[128,1,4]{2,1,0:T(2,128)(2,1)S(1)}, u32[]{:S(2)}, u32[]{:S(2)}) async-start(bf16[128,1,4]{2,1,0:T(2,128)(2,1)} %all_to_all.21), calls=%async_computation.1 | async-start | bytes 131072 | tf_op jit(solution)/shard_map/all_to_all | solution.py:105
  23.9 3.6 %scatter_custom_fusion.1 = bf16[512,2048]{1,0:T(8,128)(2,1)S(1)} fusion(s32[256]{0:T(256)S(1)} %bitcast.33, bf16[256,2048]{1,0:T(8,128)(2,1)} %param.6, bf16[]{:T(256)} %constant.177.clone.1), kind=kCustom, calls=%fused_computation.31 | custom fusion | bytes 2097664 | tf_op jit(solution)/shard_map/scatter | solution.py:92
  27.6 2.2 reshape.215
  29.8 3.7 %all-to-all-done.1 = bf16[128,1,4]{2,1,0:T(2,128)(2,1)S(1)} async-done(((bf16[128,1,4]{2,1,0:T(2,128)(2,1)}), bf16[128,1,4]{2,1,0:T(2,128)(2,1)S(1)}, u32[]{:S(2)}, u32[]{:S(2)}) %all-to-all-start.1) | async-done | bytes 1056 | tf_op jit(solution)/shard_map/all_to_all | solution.py:105
  33.4 6.1 %all-to-all-start.2 = ((bf16[128,4,2048]{2,1,0:T(4,128)(2,1)}), bf16[128,4,2048]{2,1,0:T(4,128)(2,1)S(1)}, u32[]{:S(2)}, u32[]{:S(2)}) async-start(bf16[128,4,2048]{2,1,0:T(4,128)(2,1)} %reshape.215), calls=%async_computation.2 | async-start | bytes 4194304 | tf_op jit(solution)/shard_map/all_to_all | solution.py:98
  40.4 33.1 %all-to-all-done.2 = bf16[128,4,2048]{2,1,0:T(4,128)(2,1)S(1)} async-done(((bf16[128,4,2048]{2,1,0:T(4,128)(2,1)}), bf16[128,4,2048]{2,1,0:T(4,128)(2,1)S(1)}, u32[]{:S(2)}, u32[]{:S(2)}) %all-to-all-start.2) | async-done | bytes 2097184 | tf_op jit(solution)/shard_map/all_to_all | solution.py:98
  73.5 2.1 fusion.15
  75.8 2.1 reshape.216
  77.9 6.5 %all-gather.3.cloned.1.call-done = bf16[1024,2048]{1,0:T(8,128)(2,1)} async-done(((bf16[256,2048]{1,0:T(8,128)(2,1)}), bf16[1024,2048]{1,0:T(8,128)(2,1)}) %all-gather.3.cloned.1.call-update) | async-done | bytes 4194320 | tf_op jit(solution)/shard_map/all_gather | solution.py:56
  84.4 3.6 %fusion.19 = f32[512]{0:T(512)S(1)} fusion(bf16[512,2048]{1,0:T(8,128)(2,1)} %reshape.216, f32[512]{0:T(512)S(1)} %rsqrt.18, pred[512]{0:T(512)(128)(4,1)S(1)} %gt.22), kind=kOutput, calls=%fused_computation.30 | convolution fusion | flops 1075576320 | bytes 2101760 | tf_op jit(solution)/shard_map/dot_general | solution.py:33
  88.1 17.8 %all_to_all.26 = f32[128,1,4]{2,1,0:T(1,128)S(1)} all-to-all(f32[128,1,4]{2,1,0:T(1,128)S(1)} %bitcast.29), channel_id=1, replica_groups=mesh['y'=4,'z'=4,'x'=4,'c'=2] {'y','z','x','c'}, dimensions={0} | all-to-all | bytes 4096 | tf_op jit(solution)/shard_map/all_to_all | solution.py:111
  105.9 4.3 %stack.2 = bf16[16,128,2048]{2,1,0:T(8,128)(2,1)} broadcast(bf16[128,2048]{1,0:T(8,128)(2,1)S(1)} %copy-done), dimensions={1,2} | broadcast | bytes 8912896 | tf_op jit(solution)/shard_map/stack | solution.py:58
  110.1 5.0 %all-to-all-start = ((bf16[16,128,2048]{2,1,0:T(8,128)(2,1)}), bf16[16,128,2048]{2,1,0:T(8,128)(2,1)}, u32[]{:S(2)}, u32[]{:S(2)}) async-start(bf16[16,128,2048]{2,1,0:T(8,128)(2,1)} %stack.2), calls=%async_computation | async-start | bytes 16777216 | tf_op jit(solution)/shard_map/all_to_all | solution.py:59
  115.9 12.2 %fusion.13 = f32[4,2048,512]{1,2,0:T(8,128)} fusion(s32[]{:T(128)} %bitcast.28, s32[4,512]{1,0:T(4,128)S(1)} %fusion.55, s32[2048]{0:T(1024)S(1)} %fusion.40), kind=kLoop, calls=%fused_computation.21 | loop fusion | flops 67108864 | bytes 16793604 | tf_op jit(solution)/shard_map/neg | solution.py:26
  131.4 2.5 gather_fusion
  133.9 104.4 %all-to-all-done = bf16[16,128,2048]{2,1,0:T(8,128)(2,1)} async-done(((bf16[16,128,2048]{2,1,0:T(8,128)(2,1)}), bf16[16,128,2048]{2,1,0:T(8,128)(2,1)}, u32[]{:S(2)}, u32[]{:S(2)}) %all-to-all-start) | async-done | bytes 8388640 | tf_op jit(solution)/shard_map/all_to_all | solution.py:59
  238.4 39.0 %while.11 = (s32[]{:T(128)}, f32[2048]{0:T(1024)S(1)}, bf16[4,512,2048]{2,1,0:T(8,128)(2,1)}, bf16[2048,2048]{1,0:T(8,128)(2,1)}, f32[4,2048,512]{1,2,0:T(8,128)}, /*index=5*/s32[]{:T(128)}, s32[]{:T(128)}) while((s32[]{:T(128)}, f32[2048]{0:T(1024)S(1)}, bf16[4,512,2048]{2,1,0:T(8,128)(2,1)}, bf16[2048,2048]{1,0:T(8,128)(2,1)}, ...), condition=%wide.region_2.3_spmd.clone, body=%wide.region_0.2_spmd.clone.sunk | while | flops 4298115072 | bytes 14713951 | solution.py:84
  238.4 9.7 %fusion.69 = f32[2048]{0:T(1024)S(1)} fusion(f32[4,2048,512]{1,2,0:T(8,128)} %get-tuple-element.112, s32[]{:T(128)S(6)} %copy.19, bf16[2048,2048]{1,0:T(8,128)(2,1)} %get-tuple-element.111, bf16[4,512,2048]{2,1,0:T(8,128)(2,1)} %get-tuple-element.110), kind=kOutput, calls=%fused_computation.4.clone.1 | convolution fusion | flops 4298110976 | bytes 14689280 | tf_op jit(solution)/shard_map/while/body/eval_jaxpr/dot_general | solution.py:78
  248.1 9.7 %fusion.69 = f32[2048]{0:T(1024)S(1)} fusion(f32[4,2048,512]{1,2,0:T(8,128)} %get-tuple-element.112, s32[]{:T(128)S(6)} %copy.19, bf16[2048,2048]{1,0:T(8,128)(2,1)} %get-tuple-element.111, bf16[4,512,2048]{2,1,0:T(8,128)(2,1)} %get-tuple-element.110), kind=kOutput, calls=%fused_computation.4.clone.1 | convolution fusion | flops 4298110976 | bytes 14689280 | tf_op jit(solution)/shard_map/while/body/eval_jaxpr/dot_general | solution.py:78
  257.9 9.7 %fusion.69 = f32[2048]{0:T(1024)S(1)} fusion(f32[4,2048,512]{1,2,0:T(8,128)} %get-tuple-element.112, s32[]{:T(128)S(6)} %copy.19, bf16[2048,2048]{1,0:T(8,128)(2,1)} %get-tuple-element.111, bf16[4,512,2048]{2,1,0:T(8,128)(2,1)} %get-tuple-element.110), kind=kOutput, calls=%fused_computation.4.clone.1 | convolution fusion | flops 4298110976 | bytes 14689280 | tf_op jit(solution)/shard_map/while/body/eval_jaxpr/dot_general | solution.py:78
  267.6 9.7 %fusion.69 = f32[2048]{0:T(1024)S(1)} fusion(f32[4,2048,512]{1,2,0:T(8,128)} %get-tuple-element.112, s32[]{:T(128)S(6)} %copy.19, bf16[2048,2048]{1,0:T(8,128)(2,1)} %get-tuple-element.111, bf16[4,512,2048]{2,1,0:T(8,128)(2,1)} %get-tuple-element.110), kind=kOutput, calls=%fused_computation.4.clone.1 | convolution fusion | flops 4298110976 | bytes 14689280 | tf_op jit(solution)/shard_map/while/body/eval_jaxpr/dot_general | solution.py:78
  277.3 15.2 %pmax.7 = f32[2048]{0:T(1024)S(1)} all-reduce(f32[2048]{0:T(1024)S(1)} %get-tuple-element.30), channel_id=1, replica_groups=mesh['y'=4,'z'=4,'x'=4,'c'=2] {'c','y'}, use_global_device_ids=true, to_apply=%region_3.4 | all-reduce | flops 2048 | bytes 16384 | tf_op jit(solution)/shard_map/pmax | solution.py:85
  (33 shorter events, 6.6 us)
Async XLA Ops:
  7.2 77.2 %all-gather.3.cloned.1.call-start = ((), (), s32[]{:S(2)}) async-start(), calls=%async_computation.4 | async-start | bytes 5242880 | tf_op jit(solution)/shard_map/all_gather | solution.py:56
  12.4 21.0 %all-to-all-start.1 = ((bf16[128,1,4]{2,1,0:T(2,128)(2,1)}), bf16[128,1,4]{2,1,0:T(2,128)(2,1)S(1)}, u32[]{:S(2)}, u32[]{:S(2)}) async-start(bf16[128,1,4]{2,1,0:T(2,128)(2,1)} %all_to_all.21), calls=%async_computation.1 | async-start | bytes 131072 | tf_op jit(solution)/shard_map/all_to_all | solution.py:105
  33.4 40.1 %all-to-all-start.2 = ((bf16[128,4,2048]{2,1,0:T(4,128)(2,1)}), bf16[128,4,2048]{2,1,0:T(4,128)(2,1)S(1)}, u32[]{:S(2)}, u32[]{:S(2)}) async-start(bf16[128,4,2048]{2,1,0:T(4,128)(2,1)} %reshape.215), calls=%async_computation.2 | async-start | bytes 4194304 | tf_op jit(solution)/shard_map/all_to_all | solution.py:98
  39.6 198.8 %all-gather.5.cloned.1.call-start = ((), (), s32[]{:S(2)}) async-start(), calls=%async_computation.5 | async-start | bytes 12582912 | tf_op jit(solution)/shard_map/all_gather | solution.py:55
  75.8 30.1 %copy-start = (bf16[128,2048]{1,0:T(8,128)(2,1)S(1)}, bf16[128,2048]{1,0:T(8,128)(2,1)}, u32[]{:S(2)}) copy-start(bf16[128,2048]{1,0:T(8,128)(2,1)} %param.7) | copy-start | bytes 1572868
  110.1 128.2 %all-to-all-start = ((bf16[16,128,2048]{2,1,0:T(8,128)(2,1)}), bf16[16,128,2048]{2,1,0:T(8,128)(2,1)}, u32[]{:S(2)}, u32[]{:S(2)}) async-start(bf16[16,128,2048]{2,1,0:T(8,128)(2,1)} %stack.2), calls=%async_computation | async-start | bytes 16777216 | tf_op jit(solution)/shard_map/all_to_all | solution.py:59
Sparse Core Ops, SparseCore 0:
  9.7 74.6 all-gather.2
  86.0 23.1 all-gather.4
